TPU v7x, 512 devices: a whole 4x4x16 slice. The times are simulated.
512 devices in a mesh: ctx: 64 (over x, z), head: 8 (over y, core).
Axes of the slice: x: 4, y: 4, z: 16, core: 2. Of those that a mesh axis runs over, the one named last changes fastest.
Arguments:
- query_rows: bfloat16 [8192, 6144], P('ctx', 'head'), may hold values from -6 to 6
- key_rows: bfloat16 [8192, 6144], P('ctx', 'head'), may hold values from -6 to 6
- value_rows: bfloat16 [8192, 6144], P('ctx', 'head'), may hold values from -6 to 6
- residual: bfloat16 [8192, 6144], P('ctx', 'head'), may hold values from -12 to 12
- attn_gain: float32 [6144], P('head'), may hold values from 0.5 to 1.5
- ffn_gain: float32 [6144], P('head'), may hold values from 0.5 to 1.5
- router_weight: bfloat16 [6144, 16], P('head'), may hold values from -0.078125 to 0.078125
- up_weight: bfloat16 [6144, 73728], P('head', 'ctx'), may hold values from -0.078125 to 0.078125
- down_weight: bfloat16 [73728, 6144], P('ctx', 'head'), may hold values from -0.09375 to 0.09375
- expert_ids: int32 [8192, 2], P('ctx'), may hold values from 0 to 15, as said below
Outputs:
- hidden: bfloat16 [8192, 6144], P('ctx', 'head')
- moe_out: bfloat16 [8192, 6144], P('ctx', 'head')
Inputs may be any that keep to these rules, and one draw needn't show every extreme that they name: `expert_ids`: each row names two different experts. In the rows of one device (aligned blocks of 128 rows) one expert, the same for every block, is named exactly 24 times, and every other expert (232) // 15 times or once more.
All inputs are finite; a program needn't handle non-finite values.
Results may differ from a plain program's by a relative error of at most 0.025.
Values may be sent and summed in bfloat16 or wider, within the bound.
A program may use at most 128 MiB of HBM per device.

v0:
```python
import jax
import jax.numpy as jnp
from jax import lax
from jax.sharding import PartitionSpec as P

HEAD_DIM = 128
D = 6144
EXPERTS = 16
CAP = 24


def entering(x, axis, join, neutral):
    place = lax.axis_index(axis)
    gathered = lax.all_gather(x.astype(jnp.bfloat16), axis)
    state = jnp.zeros_like(x) + jnp.asarray(neutral, x.dtype)

    def one(turn, state):
        return join(state, lax.dynamic_index_in_dim(gathered, turn, 0, False).astype(x.dtype))

    return lax.fori_loop(0, place, one, state)


def add_states(earlier, later):
    return earlier + later


def body(
    query_rows,
    key_rows,
    value_rows,
    residual,
    attn_gain,
    ffn_gain,
    router_weight,
    up_weight,
    down_weight,
    expert_ids,
):
    tok_rows, feat_width = query_rows.shape
    head_count = feat_width // HEAD_DIM
    query_heads = query_rows.reshape(tok_rows, head_count, HEAD_DIM)
    key_heads = key_rows.reshape(tok_rows, head_count, HEAD_DIM)
    value_heads = value_rows.reshape(tok_rows, head_count, HEAD_DIM)
    block_state = jnp.einsum(
        "shd,she->hde", key_heads, value_heads, preferred_element_type=jnp.float32
    )
    prior_state = entering(block_state, "ctx", add_states, jnp.zeros_like(block_state))
    causal = jnp.arange(tok_rows)[:, None] >= jnp.arange(tok_rows)[None, :]
    scores = jnp.einsum("thd,shd->hts", query_heads, key_heads, preferred_element_type=jnp.float32)
    scores = jnp.where(causal[None], scores, 0.0).astype(jnp.bfloat16)
    local_part = jnp.einsum("hts,shd->thd", scores, value_heads, preferred_element_type=jnp.float32)
    carried = jnp.einsum(
        "thd,hde->the",
        query_heads.astype(jnp.float32),
        prior_state,
        precision=lax.Precision.HIGHEST,
    )
    attn_raw = local_part + carried
    mean_sq = jnp.mean(attn_raw * attn_raw, axis=-1, keepdims=True)
    attn_norm = (attn_raw * lax.rsqrt(mean_sq + 1e-05)).reshape(tok_rows, feat_width)
    hidden = (residual.astype(jnp.float32) + attn_gain * attn_norm).astype(jnp.bfloat16)
    hidden_f = hidden.astype(jnp.float32)
    scaled = hidden_f * ffn_gain
    router_f = router_weight.astype(jnp.float32)
    total_sq = lax.psum(jnp.sum(hidden_f * hidden_f, axis=1), "head")
    inv_rms = lax.rsqrt(total_sq / D + 1e-05)[:, None]
    logits = lax.psum(jnp.dot(scaled * inv_rms, router_f, precision=lax.Precision.HIGHEST), "head")
    normed = (scaled * inv_rms).astype(jnp.bfloat16)
    expert_iota = jnp.arange(EXPERTS, dtype=jnp.int32)
    choice_hot = expert_ids[:, :, None] == expert_iota[None, None, :]
    picked = jnp.sum(jnp.where(choice_hot, logits[:, None, :], 0.0), axis=2)
    first = jax.nn.sigmoid(picked[:, 0] - picked[:, 1])
    gates = jnp.stack([first, 1.0 - first], axis=1)
    flat_hot = choice_hot.reshape(tok_rows * 2, EXPERTS).astype(jnp.int32)
    earlier = jnp.cumsum(flat_hot, axis=0) - flat_hot
    slot_rank = jnp.sum(earlier * flat_hot, axis=1).reshape(tok_rows, 2)
    position = expert_ids * CAP + slot_rank
    slot_iota = jnp.arange(EXPERTS * CAP, dtype=jnp.int32)
    landing = position[:, :, None] == slot_iota[None, None, :]
    place_table = jnp.sum(landing, axis=1).astype(jnp.bfloat16)
    outgoing = jnp.dot(place_table.T, normed, preferred_element_type=jnp.float32).astype(
        jnp.bfloat16
    )
    group_size = lax.axis_size("ctx") // EXPERTS
    outgoing = jnp.repeat(outgoing.reshape(EXPERTS, CAP, feat_width), group_size, axis=0)
    arrived = lax.all_to_all(outgoing, "ctx", split_axis=0, concat_axis=0, tiled=True)
    sources, slot_count, width_in = arrived.shape
    row_block = arrived.reshape(sources * slot_count, width_in)
    partial_value = jnp.dot(row_block, up_weight, preferred_element_type=jnp.float32)
    active = jax.nn.silu(
        lax.psum(partial_value.astype(jnp.bfloat16), "head").astype(jnp.float32)
    ).astype(jnp.bfloat16)
    part_out = jnp.dot(active, down_weight, preferred_element_type=jnp.float32).astype(jnp.bfloat16)
    expert_parts = part_out.reshape(sources, slot_count, width_in)
    returned = lax.all_to_all(expert_parts, "ctx", split_axis=0, concat_axis=0, tiled=True)
    expert_out = jnp.sum(
        returned.reshape(EXPERTS, group_size, CAP, feat_width).astype(jnp.float32), axis=1
    )
    expert_out = expert_out.reshape(EXPERTS * CAP, feat_width)
    combine_table = jnp.sum(jnp.where(landing, gates[:, :, None], 0.0), axis=1)
    moe_out = jnp.dot(combine_table, expert_out, precision=lax.Precision.HIGHEST).astype(
        jnp.bfloat16
    )
    return (hidden, moe_out)


def solution(mesh):
    placed = (
        P("ctx", "head"),
        P("ctx", "head"),
        P("ctx", "head"),
        P("ctx", "head"),
        P("head"),
        P("head"),
        P("head", None),
        P("head", "ctx"),
        P("ctx", "head"),
        P("ctx", None),
    )
    return jax.shard_map(
        body,
        mesh=mesh,
        in_specs=placed,
        out_specs=(P("ctx", "head"), P("ctx", "head")),
        check_vma=False,
    )
```

profile of v0, /device:TPU:25, one launch (start us, length us, event | category | flops | bytes accessed | tf_op | source)
XLA Modules:
  0.0 607.4 jit_solution(4907155735518995915)
XLA Ops:
  7.2 1.2 copy.68
  8.4 1.1 copy.71
  9.5 0.9 convolution_convert_fusion.3
  10.6 0.8 copy.76
  11.6 1.1 copy.67
  12.7 0.6 reduce-window.6
  13.9 0.6 copy-done.3
  14.6 170.1 %all-gather.3.cloned.1.call-done = bf16[384,128,128]{2,1,0:T(8,128)(2,1)} async-done(((bf16[6,128,128]{2,1,0:T(8,128)(2,1)}), bf16[384,128,128]{2,1,0:T(8,128)(2,1)}) %all-gather.3.cloned.1.call-update) | async-done | bytes 12582928 | tf_op jit(solution)/shard_map/all_gather | solution.py:14
  184.8 0.5 convolution_bitcast_fusion
  185.3 1.0 multiply_reduce_fusion
  186.3 0.7 add_rsqrt_fusion
  187.2 0.8 fusion.15
  188.1 12.1 %psum.21 = f32[128]{0:T(128)S(1)} all-reduce(f32[128]{0:T(128)S(1)} %get-tuple-element.36), channel_id=1, replica_groups=mesh['ctx'=64,'head'=8] {'head'}, use_global_device_ids=true, to_apply=%region_7.8 | all-reduce | flops 128 | bytes 1024 | tf_op jit(solution)/shard_map/psum | solution.py:65
  200.2 0.4 convolution_convert_fusion.1
  200.7 179.5 %all_to_all.10 = bf16[64,24,768]{2,1,0:T(8,128)(2,1)S(1)} all-to-all(bf16[64,24,768]{2,1,0:T(8,128)(2,1)S(1)} %bitcast.56), channel_id=1, replica_groups=mesh['ctx'=64,'head'=8] {'ctx'}, dimensions={0} | all-to-all | bytes 4718592 | tf_op jit(solution)/shard_map/all_to_all | solution.py:86
  380.3 4.7 convolution_convert_fusion
  385.0 78.6 %all-reduce.2.cloned.1.call-done = bf16[1536,1152]{1,0:T(8,128)(2,1)} async-done(((bf16[1536,1152]{1,0:T(8,128)(2,1)}), bf16[1536,1152]{1,0:T(8,128)(2,1)}) %all-reduce.2.cloned.1.call-update) | async-done | bytes 3538960 | tf_op jit(solution)/shard_map/psum | solution.py:91
  463.6 8.1 %fusion.6 = bf16[1536,768]{1,0:T(8,128)(2,1)} fusion(bf16[1152,768]{1,0:T(8,128)(2,1)} %param.20, bf16[1536,1152]{1,0:T(8,128)(2,1)} %all-reduce.2.cloned.1.call-done), kind=kOutput, calls=%fused_computation.10 | convolution fusion | flops 2729705472 | bytes 7667712 | tf_op jit(solution)/shard_map/dot_general | solution.py:93
  471.7 15.7 %all-to-all-start.1 = ((bf16[64,24,768]{2,1,0:T(8,128)(2,1)}), bf16[64,24,768]{2,1,0:T(8,128)(2,1)}, u32[]{:S(2)}, u32[]{:S(2)}) async-start(bf16[64,24,768]{2,1,0:T(8,128)(2,1)} %bitcast.58), calls=%async_computation.1 | async-start | bytes 4718592 | tf_op jit(solution)/shard_map/all_to_all | solution.py:95
  487.5 0.3 fusion.13
  487.8 13.0 %psum.22 = f32[128,16]{0,1:T(8,128)S(1)} all-reduce(f32[128,16]{0,1:T(8,128)S(1)} %fusion.13), channel_id=1, replica_groups=mesh['ctx'=64,'head'=8] {'head'}, use_global_device_ids=true, to_apply=%region_8.9 | all-reduce | flops 2048 | bytes 16384 | tf_op jit(solution)/shard_map/psum | solution.py:67
  501.0 95.9 %all-to-all-done.1 = bf16[64,24,768]{2,1,0:T(8,128)(2,1)} async-done(((bf16[64,24,768]{2,1,0:T(8,128)(2,1)}), bf16[64,24,768]{2,1,0:T(8,128)(2,1)}, u32[]{:S(2)}, u32[]{:S(2)}) %all-to-all-start.1) | async-done | bytes 2359328 | tf_op jit(solution)/shard_map/all_to_all | solution.py:95
  596.8 2.2 convert_reduce_fusion
  599.0 1.6 convolution_convert_fusion.2
  (43 shorter events, 1.7 us)
Async XLA Ops:
  7.2 373.1 %copy-start = (bf16[768,1152]{1,0:T(8,128)(2,1)S(1)}, bf16[768,1152]{1,0:T(8,128)(2,1)}, u32[]{:S(2)}) copy-start(bf16[768,1152]{1,0:T(8,128)(2,1)} %param.19) | copy-start | bytes 5308420
  7.2 6.7 %copy-start.5 = (s32[128,2]{0,1:T(2,128)S(1)}, s32[128,2]{0,1:T(2,128)}, u32[]{:S(2)}) copy-start(s32[128,2]{0,1:T(2,128)} %param.21) | copy-start | bytes 3076
  7.2 177.5 %all-gather.3.cloned.1.call-start = ((), (), s32[]{:S(2)}) async-start(), calls=%async_computation.3 | async-start | bytes 12779520 | tf_op jit(solution)/shard_map/all_gather | solution.py:14
  10.5 453.1 %all-reduce.2.cloned.1.call-start = ((), (), s32[]{:S(2)}) async-start(), calls=%async_computation.2 | async-start | bytes 7077888 | tf_op jit(solution)/shard_map/psum | solution.py:91
  13.9 0.6 copy-start.3
  184.7 2.5 copy-start.2
  186.3 13.9 %copy-start.7 = (f32[768]{0:T(1024)S(1)}, f32[768]{0:T(1024)}, u32[]{:S(2)}) copy-start(f32[768]{0:T(1024)} %param.17) | copy-start | bytes 9220
  188.1 299.4 %copy-start.1 = (bf16[128,768]{1,0:T(8,128)(2,1)}, bf16[128,768]{1,0:T(8,128)(2,1)S(1)}, u32[]{:S(2)}) copy-start(bf16[128,768]{1,0:T(8,128)(2,1)S(1)} %get-tuple-element.37) | copy-start | bytes 589828
  471.7 15.7 %copy-start.8 = (bf16[768,16]{0,1:T(8,128)(2,1)S(1)}, bf16[768,16]{0,1:T(8,128)(2,1)}, u32[]{:S(2)}) copy-start(bf16[768,16]{0,1:T(8,128)(2,1)} %param.18) | copy-start | bytes 73732
  471.7 29.0 %copy-start.6 = (s32[128,2]{0,1:T(2,128)S(1)}, s32[128,2]{0,1:T(2,128)}, u32[]{:S(2)}) copy-start(s32[128,2]{0,1:T(2,128)} %param.21) | copy-start | bytes 3076
  471.7 29.1 %copy-start.4 = (s32[128,2]{0,1:T(2,128)S(1)}, s32[128,2]{0,1:T(2,128)}, u32[]{:S(2)}) copy-start(s32[128,2]{0,1:T(2,128)} %copy-done.3) | copy-start | bytes 3076
  471.7 125.1 %all-to-all-start.1 = ((bf16[64,24,768]{2,1,0:T(8,128)(2,1)}), bf16[64,24,768]{2,1,0:T(8,128)(2,1)}, u32[]{:S(2)}, u32[]{:S(2)}) async-start(bf16[64,24,768]{2,1,0:T(8,128)(2,1)} %bitcast.58), calls=%async_computation.1 | async-start | bytes 4718592 | tf_op jit(solution)/shard_map/all_to_all | solution.py:95
Sparse Core Ops, SparseCore 0:
  11.5 173.1 all-gather.2
  385.1 78.4 all-reduce.1
where the time goes:
time: 609 us; the launch traced here: 607 us
  waiting for transfers between devices  345 us (57%)
  blocking collectives  205 us (34%)
  matrix products  17.5 us (3%)
  starting transfers between devices  15.8 us (3%)
  between operations  14.3 us (2%)
    all_to_all x1, blocking collectives, body(): lax.all_to_all(outgoing, 'ctx', split_axis=0, concat_axis=0, tiled=True)  180 us
    all_gather x1, waiting for transfers between devices, entering(): gathered = lax.all_gather(x.astype(jnp.bfloat16), axis)  170 us
    all_to_all x1, waiting for transfers between devices, body(): lax.all_to_all(expert_parts, 'ctx', split_axis=0, concat_axis=0, tiled=True)  95.9 us
    psum x1, waiting for transfers between devices, body(): lax.psum(partial_value.astype(jnp.bfloat16), 'head').astype(jnp.float32)  78.6 us
    all_to_all x1, starting transfers between devices, body(): lax.all_to_all(expert_parts, 'ctx', split_axis=0, concat_axis=0, tiled=True)  15.7 us
    psum x1, blocking collectives, body(): lax.psum(jnp.dot(scaled * inv_rms, router_f, precision=lax.Precision.HIGH...  13 us
  transfers between devices with their start and end apart: 3, of which 3 were waited for; matrix products, arithmetic and copies ran while one was open for 1% of the time, Pallas kernels for 0%

commit v1 on v0

v1 whole, which is shorter than its diff:
```python
import jax
import jax.numpy as jnp
from jax import lax
from jax.experimental import pallas as pl
from jax.experimental.pallas import tpu as pltpu
from jax.sharding import PartitionSpec as P

HEAD_DIM = 128
D = 6144
EXPERTS = 16
CAP = 24
NX = 4
NZ = 16
NY = 4
MESH = pl.DeviceIdType.MESH
F32 = jnp.float32
BF16 = jnp.bfloat16
HIGHEST = lax.Precision.HIGHEST


def spot():
    ctx = lax.axis_index("ctx")
    head = lax.axis_index("head")
    return ctx // NZ, ctx % NZ, head // 2, head % 2


def send(src, dst, send_sem, recv_sem, ctx, head):
    copy = pltpu.make_async_remote_copy(
        src_ref=src,
        dst_ref=dst,
        send_sem=send_sem,
        recv_sem=recv_sem,
        device_id=(ctx, head),
        device_id_type=MESH,
    )
    copy.start()
    return copy


def await_bytes(ref, sem):
    pltpu.make_async_copy(ref, ref, sem).wait()


def greet(barrier, ctx, head):
    pl.semaphore_signal(barrier, inc=1, device_id=(ctx, head), device_id_type=MESH)


def dot(a, b, dims, precision=None):
    return lax.dot_general(a, b, (dims, ((), ())), precision=precision, preferred_element_type=F32)


def attend(
    ids_ref,
    query_ref,
    key_ref,
    value_ref,
    residual_ref,
    attn_gain_ref,
    ffn_gain_ref,
    router_ref,
    up_ref,
    down_ref,
    hidden_ref,
    outgoing_ref,
    meta_ref,
    up_other_ref,
    down_other_ref,
    state,
    landed,
    total,
    totals,
    before,
    answer,
    prior,
    local,
    stats,
    all_stats,
    weight_send,
    weight_recv,
    state_send,
    state_recv,
    total_send,
    total_recv,
    answer_send,
    answer_recv,
    stat_send,
    stat_recv,
):
    x, z, y, core = spot()
    ctx = x * NZ + z
    head = y * 2 + core
    heads = query_ref.shape[1] // HEAD_DIM
    rows = query_ref.shape[0]
    part = heads * HEAD_DIM // NZ

    barrier = pltpu.get_barrier_semaphore()
    for dz in range(1, NZ):
        greet(barrier, x * NZ + (z + dz) % NZ, head)
    for dx in range(1, NX):
        greet(barrier, ((x + dx) % NX) * NZ + z, head)
    for dh in range(1, 8):
        greet(barrier, ctx, (head + dh) % 8)

    for h in range(heads):
        cols = slice(h * HEAD_DIM, (h + 1) * HEAD_DIM)
        state[cols, :] = dot(key_ref[:, cols], value_ref[:, cols], ((0,), (0,))).astype(BF16)

    pl.semaphore_wait(barrier, 25)

    def slab(index):
        return pl.ds(pl.multiple_of(index * part, 16), part)

    state_copies = []
    for dz in range(1, NZ):
        other = (z + dz) % NZ
        state_copies.append(
            send(state.at[slab(other)], landed.at[z], state_send, state_recv, x * NZ + other, head)
        )
    mate = y * 2 + 1 - core
    up_copy = send(up_ref, up_other_ref, weight_send.at[0], weight_recv.at[0], ctx, mate)
    down_copy = send(down_ref, down_other_ref, weight_send.at[1], weight_recv.at[1], ctx, mate)

    landed[z] = state[slab(z), :]
    row_iota = lax.broadcasted_iota(jnp.int32, (rows, rows), 0)
    col_iota = lax.broadcasted_iota(jnp.int32, (rows, rows), 1)
    for h in range(heads):
        cols = slice(h * HEAD_DIM, (h + 1) * HEAD_DIM)
        scores = dot(query_ref[:, cols], key_ref[:, cols], ((1,), (1,)))
        scores = jnp.where(row_iota >= col_iota, scores, 0.0).astype(BF16)
        local[:, cols] = dot(scores, value_ref[:, cols], ((1,), (0,)))

    await_bytes(landed.at[pl.ds(0, NZ - 1)], state_recv)
    running = jnp.zeros((part, HEAD_DIM), F32)
    for turn in range(NZ):
        before[turn] = running
        running = running + landed[turn].astype(F32)
    total[...] = running
    for dx in range(1, NX):
        other = (x + dx) % NX
        send(total, totals.at[x], total_send, total_recv, other * NZ + z, head)
    await_bytes(totals.at[pl.ds(0, NX - 1)], total_recv)
    base = jnp.zeros((part, HEAD_DIM), F32)
    for turn in range(NX - 1):
        base = base + jnp.where(turn < x, totals[turn], 0.0)
    for turn in range(NZ):
        answer[turn] = (before[turn] + base).astype(BF16)
    for dz in range(1, NZ):
        other = (z + dz) % NZ
        send(answer.at[other], prior.at[slab(z)], answer_send, answer_recv, x * NZ + other, head)
    prior[slab(z), :] = answer[z]

    eye = row_iota == col_iota
    ids = ids_ref[...]
    row_ids = [
        jnp.sum(jnp.where(eye, ids[:, k : k + 1], 0), axis=0, keepdims=True) for k in range(2)
    ]
    expert_iota = lax.broadcasted_iota(jnp.int32, (EXPERTS, rows), 0)
    hots = [expert_iota == row for row in row_ids]
    both = (hots[0] | hots[1]).astype(F32).astype(BF16)
    strict = (row_iota < col_iota).astype(F32).astype(BF16)
    counts = dot(both, strict, ((1,), (0,)))
    places = [
        row.astype(F32) * CAP + jnp.sum(jnp.where(hot, counts, 0.0), axis=0, keepdims=True)
        for row, hot in zip(row_ids, hots)
    ]

    await_bytes(answer.at[pl.ds(0, NZ - 1)], answer_recv)
    for h in range(heads):
        cols = slice(h * HEAD_DIM, (h + 1) * HEAD_DIM)
        raw = local[:, cols] + dot(query_ref[:, cols], prior[cols, :], ((1,), (0,)))
        mean_sq = jnp.mean(raw * raw, axis=-1, keepdims=True)
        normal = raw * lax.rsqrt(mean_sq + 1e-05)
        hidden_ref[:, cols] = (
            residual_ref[:, cols].astype(F32) + attn_gain_ref[:, cols] * normal
        ).astype(BF16)
    hidden = hidden_ref[...].astype(F32)
    scaled = hidden * ffn_gain_ref[...]
    ones = jnp.ones((8, hidden.shape[1]), F32)
    stats[0:EXPERTS, :] = dot(router_ref[...].astype(F32), scaled, ((1,), (1,)), HIGHEST)
    stats[EXPERTS : EXPERTS + 8, :] = dot(ones, hidden * hidden, ((1,), (1,)), HIGHEST)
    for dh in range(1, 8):
        send(stats, all_stats.at[head], stat_send, stat_recv, ctx, (head + dh) % 8)
    all_stats[head] = stats[...]
    await_bytes(all_stats.at[pl.ds(0, 7)], stat_recv)
    summed = all_stats[0]
    for turn in range(1, 8):
        summed = summed + all_stats[turn]
    inv_row = lax.rsqrt(summed[EXPERTS : EXPERTS + 1, :] / D + 1e-05)
    logits = summed[0:EXPERTS, :] * inv_row
    picked = [jnp.sum(jnp.where(hot, logits, 0.0), axis=0, keepdims=True) for hot in hots]
    first = jax.nn.sigmoid(picked[0] - picked[1])
    meta_ref[...] = jnp.concatenate(
        [places[0], places[1], first, 1.0 - first, jnp.zeros((4, rows), F32)], axis=0
    )
    inv_col = jnp.sum(jnp.where(eye, inv_row, 0.0), axis=1, keepdims=True)
    normed = (scaled * inv_col).astype(BF16)
    slot_iota = lax.broadcasted_iota(jnp.int32, (EXPERTS * CAP, rows), 0).astype(F32)
    table = ((slot_iota == places[0]) | (slot_iota == places[1])).astype(F32).astype(BF16)
    outgoing_ref[...] = dot(table, normed, ((1,), (0,))).astype(BF16)

    await_bytes(landed.at[pl.ds(0, NZ - 1)], state_send)
    await_bytes(totals.at[pl.ds(0, NX - 1)], total_send)
    await_bytes(answer.at[pl.ds(0, NZ - 1)], answer_send)
    await_bytes(all_stats.at[pl.ds(0, 7)], stat_send)
    up_copy.wait()
    down_copy.wait()


def run_attend(ids, query, key, value, residual, attn_gain, ffn_gain, router, up, down):
    rows, width = query.shape
    part = width // NZ
    vmem = pl.BlockSpec(memory_space=pltpu.VMEM)
    anywhere = pl.BlockSpec(memory_space=pl.ANY)
    dma = pltpu.SemaphoreType.DMA
    return pl.pallas_call(
        attend,
        out_shape=(
            jax.ShapeDtypeStruct((rows, width), BF16),
            jax.ShapeDtypeStruct((EXPERTS * CAP, width), BF16),
            jax.ShapeDtypeStruct((8, rows), F32),
            jax.ShapeDtypeStruct(up.shape, BF16),
            jax.ShapeDtypeStruct(down.shape, BF16),
        ),
        in_specs=[vmem] * 8 + [anywhere] * 2,
        out_specs=(vmem, vmem, vmem, anywhere, anywhere),
        scratch_shapes=[
            pltpu.VMEM((width, HEAD_DIM), BF16),
            pltpu.VMEM((NZ, part, HEAD_DIM), BF16),
            pltpu.VMEM((part, HEAD_DIM), F32),
            pltpu.VMEM((NX, part, HEAD_DIM), F32),
            pltpu.VMEM((NZ, part, HEAD_DIM), F32),
            pltpu.VMEM((NZ, part, HEAD_DIM), BF16),
            pltpu.VMEM((width, HEAD_DIM), BF16),
            pltpu.VMEM((rows, width), F32),
            pltpu.VMEM((EXPERTS + 8, rows), F32),
            pltpu.VMEM((8, EXPERTS + 8, rows), F32),
            dma((2,)),
            dma((2,)),
            dma,
            dma,
            dma,
            dma,
            dma,
            dma,
            dma,
            dma,
        ],
        compiler_params=pltpu.CompilerParams(
            collective_id=0, has_side_effects=True, vmem_limit_bytes=48 * 1024 * 1024
        ),
        name="attend",
    )(ids, query, key, value, residual, attn_gain, ffn_gain, router, up, down)


def body(
    query_rows,
    key_rows,
    value_rows,
    residual,
    attn_gain,
    ffn_gain,
    router_weight,
    up_weight,
    down_weight,
    expert_ids,
):
    tok_rows, feat_width = query_rows.shape
    hidden, outgoing, meta, up_other, down_other = run_attend(
        expert_ids,
        query_rows,
        key_rows,
        value_rows,
        residual,
        attn_gain[None, :],
        ffn_gain[None, :],
        router_weight.T,
        up_weight,
        down_weight,
    )
    slot_iota = jnp.arange(EXPERTS * CAP, dtype=jnp.int32).astype(F32)[None, :]
    combine_table = jnp.where(slot_iota == meta[0][:, None], meta[2][:, None], 0.0) + jnp.where(
        slot_iota == meta[1][:, None], meta[3][:, None], 0.0
    )
    group_size = lax.axis_size("ctx") // EXPERTS
    outgoing = jnp.repeat(outgoing.reshape(EXPERTS, CAP, feat_width), group_size, axis=0)
    arrived = lax.all_to_all(outgoing, "ctx", split_axis=0, concat_axis=0, tiled=True)
    sources, slot_count, width_in = arrived.shape
    row_block = arrived.reshape(sources * slot_count, width_in)
    partial_value = jnp.dot(row_block, up_weight, preferred_element_type=jnp.float32)
    active = jax.nn.silu(
        lax.psum(partial_value.astype(jnp.bfloat16), "head").astype(jnp.float32)
    ).astype(jnp.bfloat16)
    part_out = jnp.dot(active, down_weight, preferred_element_type=jnp.float32).astype(jnp.bfloat16)
    expert_parts = part_out.reshape(sources, slot_count, width_in)
    returned = lax.all_to_all(expert_parts, "ctx", split_axis=0, concat_axis=0, tiled=True)
    expert_out = jnp.sum(
        returned.reshape(EXPERTS, group_size, CAP, feat_width).astype(jnp.float32), axis=1
    )
    expert_out = expert_out.reshape(EXPERTS * CAP, feat_width)
    moe_out = jnp.dot(combine_table, expert_out, precision=lax.Precision.HIGHEST).astype(
        jnp.bfloat16
    )
    return (hidden, moe_out)


def solution(mesh):
    placed = (
        P("ctx", "head"),
        P("ctx", "head"),
        P("ctx", "head"),
        P("ctx", "head"),
        P("head"),
        P("head"),
        P("head", None),
        P("head", "ctx"),
        P("ctx", "head"),
        P("ctx", None),
    )
    return jax.shard_map(
        body,
        mesh=mesh,
        in_specs=placed,
        out_specs=(P("ctx", "head"), P("ctx", "head")),
        check_vma=False,
    )
```

time: 609 us -> 405 us (0.67)
  waiting for transfers between devices: 345 us -> 189 us
  blocking collectives: 205 us -> 115 us
  Pallas kernels: 0 us -> 49.2 us
    all_gather x1 -> x0, waiting for transfers between devices: 170 us -> none  [entering(): gathered = lax.all_gather(x.astype(jnp.bfloat16), axis)]
    all_to_all x1, blocking collectives: 180 us -> 115 us  [body(): lax.all_to_all(outgoing, 'ctx', split_axis=0, concat_axis=0, tiled=True)]
    pallas_call x0 -> x1, Pallas kernels: none -> 49.2 us  [run_attend(): pl.pallas_call(attend, out_shape=(jax.ShapeDtypeStruct((rows, width), BF1...]
    psum x2 -> x0, blocking collectives: 25.1 us -> none  [the longest x1 13 us: body(): lax.psum(jnp.dot(scaled * inv_rms, router_f, precision=lax.Precision.HIGH...]
    all_to_all x1, waiting for transfers between devices: 95.9 us -> 110 us  [body(): lax.all_to_all(expert_parts, 'ctx', split_axis=0, concat_axis=0, tiled=True)]
  transfers between devices with their start and end apart: 3 -> 2, of which waited for: 3 -> 2; matrix products, arithmetic and copies ran while one was open for 1% -> 0% of each run, Pallas kernels for 0% -> 0%
where the time goes in v1:
time: 405 us; the launch traced here: 404 us
  waiting for transfers between devices  189 us (47%)
  blocking collectives  115 us (28%)
  Pallas kernels  49.2 us (12%)
  starting transfers between devices  15.4 us (4%)
  between operations  14.1 us (3%)
  matrix products  13.8 us (3%)
  local copies, waits for them, and re-layouts  7.45 us (2%)
    all_to_all x1, blocking collectives, body(): lax.all_to_all(outgoing, 'ctx', split_axis=0, concat_axis=0, tiled=True)  115 us
    all_to_all x1, waiting for transfers between devices, body(): lax.all_to_all(expert_parts, 'ctx', split_axis=0, concat_axis=0, tiled=True)  110 us
    psum x1, waiting for transfers between devices, body(): lax.psum(partial_value.astype(jnp.bfloat16), 'head').astype(jnp.float32)  79 us
    pallas_call x1, Pallas kernels, run_attend(): pl.pallas_call(attend, out_shape=(jax.ShapeDtypeStruct((rows, width), BF1...  49.2 us
    all_to_all x1, starting transfers between devices, body(): lax.all_to_all(expert_parts, 'ctx', split_axis=0, concat_axis=0, tiled=True)  15.3 us
  transfers between devices with their start and end apart: 2, of which 2 were waited for; matrix products, arithmetic and copies ran while one was open for 0% of the time, Pallas kernels for 0%

profile of v1, /device:TPU:25, one launch (start us, length us, event | category | flops | bytes accessed | tf_op | source)
XLA Modules:
  0.0 404.1 jit_solution(5972443564401944927)
XLA Ops:
  7.2 0.0 all-reduce.2.cloned.1.call-start
  7.2 0.8 copy.12.ids_ref
  8.0 0.7 broadcast_in_dim.32.attn_gain_ref
  8.7 0.7 broadcast_in_dim.33.ffn_gain_ref
  9.4 0.9 copy-done
  10.3 0.9 copy-done.1
  11.2 0.9 copy-done.2
  12.2 0.9 copy-done.3
  13.1 0.7 copy-done.4
  13.8 49.2 %attend.1 = (bf16[128,768]{1,0:T(8,128)(2,1)S(1)}, bf16[384,768]{1,0:T(8,128)(2,1)S(1)}, f32[8,128]{1,0:T(8,128)S(1)}, bf16[768,1152]{1,0:T(8,128)(2,1)}, bf16[1152,768]{1,0:T(8,128)(2,1)}) custom-call(s32[128,2]{1,0:T(8,128)S(1)} %copy.12.ids_ref, bf16[128,768]{1,0:T(8,128)(2,1)S(1)} %copy-done, bf16[128,768]{1,0:T(8,128)(2,1)S(1)} %copy-done.1, ...), custom_call_target="tpu_custom_call" | custom-call | tf_op jit(solution)/shard_map/attend/pallas_call | solution.py:215
  63.1 0.2 broadcast_in_dim.39
  63.2 0.0 copy-start.5
  63.2 115.3 %all_to_all.10 = bf16[64,24,768]{2,1,0:T(8,128)(2,1)S(1)} all-to-all(bf16[64,24,768]{2,1,0:T(8,128)(2,1)S(1)} %bitcast.23), channel_id=1, replica_groups=mesh['ctx'=64,'head'=8] {'ctx'}, dimensions={0} | all-to-all | bytes 4718592 | tf_op jit(solution)/shard_map/all_to_all | solution.py:286
  178.5 0.0 copy-done.5
  178.5 4.6 %convolution_convert_fusion = bf16[1536,1152]{1,0:T(8,128)(2,1)} fusion(bf16[1536,768]{1,0:T(8,128)(2,1)S(1)} %bitcast.26, bf16[768,1152]{1,0:T(8,128)(2,1)S(1)} %copy-done.5), kind=kOutput, calls=%fused_computation.2 | convolution fusion | flops 2719678464 | bytes 7667712 | tf_op jit(solution)/shard_map/dot_general | solution.py:289
  183.2 0.0 all-reduce.2.cloned.1.call-update
  183.2 79.0 %all-reduce.2.cloned.1.call-done = bf16[1536,1152]{1,0:T(8,128)(2,1)} async-done(((bf16[1536,1152]{1,0:T(8,128)(2,1)}), bf16[1536,1152]{1,0:T(8,128)(2,1)}) %all-reduce.2.cloned.1.call-update) | async-done | bytes 3538960 | tf_op jit(solution)/shard_map/psum | solution.py:291
  262.2 0.0 copy-done.6
  262.2 7.6 %fusion.6 = bf16[1536,768]{1,0:T(8,128)(2,1)} fusion(bf16[1152,768]{1,0:T(8,128)(2,1)S(1)} %copy-done.6, bf16[1536,1152]{1,0:T(8,128)(2,1)} %all-reduce.2.cloned.1.call-done), kind=kOutput, calls=%fused_computation.9 | convolution fusion | flops 2729705472 | bytes 7667712 | tf_op jit(solution)/shard_map/dot_general | solution.py:293
  269.8 15.3 %all-to-all-start.1 = ((bf16[64,24,768]{2,1,0:T(8,128)(2,1)}), bf16[64,24,768]{2,1,0:T(8,128)(2,1)S(1)}, u32[]{:S(2)}, u32[]{:S(2)}) async-start(bf16[64,24,768]{2,1,0:T(8,128)(2,1)} %bitcast.25), calls=%async_computation.1 | async-start | bytes 4718592 | tf_op jit(solution)/shard_map/all_to_all | solution.py:295
  285.1 109.5 %all-to-all-done.1 = bf16[64,24,768]{2,1,0:T(8,128)(2,1)S(1)} async-done(((bf16[64,24,768]{2,1,0:T(8,128)(2,1)}), bf16[64,24,768]{2,1,0:T(8,128)(2,1)S(1)}, u32[]{:S(2)}, u32[]{:S(2)}) %all-to-all-start.1) | async-done | bytes 2359328 | tf_op jit(solution)/shard_map/all_to_all | solution.py:295
  394.6 0.4 convert_reduce_fusion
  395.0 1.6 convolution_convert_fusion.1
  396.6 0.7 copy.15
  (8 shorter events, 0.0 us)
Async XLA Ops:
  7.2 255.0 %all-reduce.2.cloned.1.call-start = ((), (), s32[]{:S(2)}) async-start(), calls=%async_computation.2 | async-start | bytes 7077888 | tf_op jit(solution)/shard_map/psum | solution.py:291
  9.4 0.9 copy-start
  10.3 0.9 copy-start.1
  11.2 0.9 copy-start.2
  12.2 0.9 copy-start.3
  13.1 0.7 copy-start.4
  63.2 115.3 %copy-start.5 = (bf16[768,1152]{1,0:T(8,128)(2,1)S(1)}, bf16[768,1152]{1,0:T(8,128)(2,1)}, u32[]{:S(2)}) copy-start(bf16[768,1152]{1,0:T(8,128)(2,1)} %up_ref.1) | copy-start | bytes 5308420
  183.2 79.0 %copy-start.6 = (bf16[1152,768]{1,0:T(8,128)(2,1)S(1)}, bf16[1152,768]{1,0:T(8,128)(2,1)}, u32[]{:S(2)}) copy-start(bf16[1152,768]{1,0:T(8,128)(2,1)} %down_ref.1) | copy-start | bytes 5308420
  269.8 124.9 %all-to-all-start.1 = ((bf16[64,24,768]{2,1,0:T(8,128)(2,1)}), bf16[64,24,768]{2,1,0:T(8,128)(2,1)S(1)}, u32[]{:S(2)}, u32[]{:S(2)}) async-start(bf16[64,24,768]{2,1,0:T(8,128)(2,1)} %bitcast.25), calls=%async_computation.1 | async-start | bytes 4718592 | tf_op jit(solution)/shard_map/all_to_all | solution.py:295
Sparse Core Ops, SparseCore 0:
  183.3 78.8 all-reduce.1
